TPU v7x, 256 devices: a whole 4x4x8 slice. The times are simulated.
256 devices in a mesh: gx: 32 (over x, z), gy: 8 (over y, core).
Axes of the slice: x: 4, y: 4, z: 8, core: 2. Of those that a mesh axis runs over, the one named last changes fastest.
Arguments:
- features: bfloat16 [2097152, 64], P(('gx', 'gy')), may hold values from -6 to 6
- conv_weight: bfloat16 [27, 64, 64], replicated, may hold values from -0.15625 to 0.15625
- down_weight: bfloat16 [8, 64, 128], replicated, may hold values from -0.375 to 0.375
- kernel_map: int32 [27, 16384], P(None, ('gx', 'gy')), may hold values from 0 to 128, as said below
- halo_rows: int32 [8, 2048], P(None, ('gx', 'gy')), may hold values from 0 to 63
- send_rows: int32 [32, 131072], P(None, ('gx', 'gy')), may hold values from 0 to 8192, as said below
- send_sub: int32 [32, 131072], P(None, ('gx', 'gy')), may hold values from 0 to 7
- recv_coarse: int32 [32, 131072], P(None, ('gx', 'gy')), may hold values from 0 to 2047
Outputs:
- refined: bfloat16 [2097152, 64], P(('gx', 'gy'))
- coarse: bfloat16 [524288, 128], P(('gx', 'gy'))
Inputs may be any that keep to these rules, and one draw needn't show every extreme that they name: `kernel_map`: entries below 64 name local blocks, the next 64 name the received blocks of directions 0 to 7 in order, 128 means no neighbour; offset 13 maps every block to itself. `send_rows`: each local row below 8192 stands in exactly one slot of its slab; 8192 marks an empty slot; one hash owner of each slab gets all 512 of its slots filled.
All inputs are finite; a program needn't handle non-finite values.
Results may differ from a plain program's by a relative error of at most 0.0047.
Values may be sent and summed in bfloat16 or wider, within the bound.
A program may use at most 128 MiB of HBM per device.

v0:
```python
import math

import jax
import jax.numpy as jnp
from jax import lax
from jax.sharding import PartitionSpec as P

BLOCK = 128


def shifted(block, axis, distance):
    devices = range(lax.axis_size(axis))
    route = [(i - distance, i) for i in devices if i - distance in devices]
    return lax.ppermute(block, axis, route)


def block_convolve_step(table_blocks, offsets, weights):
    picked = table_blocks[offsets]
    return jnp.einsum("kgbc,kcd->gbd", picked, weights, preferred_element_type=jnp.float32)


def sub_products(rows, sub_codes, weights):
    total = rows.shape[0]
    step_rows = math.gcd(total, 512)
    grouped_rows = rows.reshape(total // step_rows, step_rows, rows.shape[1])
    grouped_codes = sub_codes.reshape(total // step_rows, step_rows)

    def product_group(operands):
        group_rows, group_codes = operands
        every_sub = jnp.einsum(
            "rc,scd->rsd", group_rows, weights, preferred_element_type=jnp.float32
        )
        return jnp.take_along_axis(every_sub, group_codes[:, None, None], axis=1)[:, 0]

    result = lax.map(product_group, (grouped_rows, grouped_codes))
    return result.reshape(total, weights.shape[2])


def on_device(
    features, conv_weight, down_weight, kernel_map, halo_rows, send_rows, send_sub, recv_coarse
):
    voxels, channels = features.shape
    halo_count = halo_rows.shape[1] * BLOCK
    flat_width = halo_count * channels
    feature_blocks = features.reshape(voxels // BLOCK, BLOCK, channels)
    outgoing = feature_blocks[halo_rows].reshape(8, flat_width)
    from_below = shifted(outgoing[5:8], "gx", 1)
    upper_incoming = shifted(outgoing[0:3], "gx", -1)
    sectioned = jnp.concatenate([upper_incoming, outgoing[3:5], from_below], axis=0)
    rising = shifted(jnp.stack([sectioned[2], sectioned[4], sectioned[7]]), "gy", 1)
    falling = shifted(jnp.stack([sectioned[0], sectioned[3], sectioned[5]]), "gy", -1)
    arrived = jnp.stack(
        [
            falling[0],
            sectioned[1],
            rising[0],
            falling[1],
            rising[1],
            falling[2],
            sectioned[6],
            rising[2],
        ]
    )
    lookup_table = jnp.concatenate(
        [
            features,
            arrived.reshape(8 * halo_count, channels),
            jnp.zeros((BLOCK, channels), features.dtype),
        ],
        axis=0,
    )
    table_blocks = lookup_table.reshape(-1, BLOCK, channels)
    block_total = voxels // BLOCK
    group = math.gcd(block_total, max(1, 2048 // BLOCK))
    offset_groups = kernel_map.reshape(kernel_map.shape[0], block_total // group, group).transpose(
        1, 0, 2
    )
    summed_conv = lax.map(
        lambda offsets: block_convolve_step(table_blocks, offsets, conv_weight), offset_groups
    )
    refined = jax.nn.relu(summed_conv.reshape(voxels, channels)).astype(jnp.bfloat16)
    peers, capacity = send_rows.shape
    padded_fine = jnp.concatenate([refined, jnp.zeros((1, channels), jnp.bfloat16)], axis=0)
    slot_rows = padded_fine[send_rows.reshape(-1)]
    out_width = down_weight.shape[2]
    coarse_count = voxels // 4
    contributions = sub_products(slot_rows, send_sub.reshape(-1), down_weight).reshape(
        peers, capacity, out_width
    )
    landed = lax.all_to_all(contributions, "gx", split_axis=0, concat_axis=0, tiled=True).reshape(
        -1, out_width
    )
    coarse = jax.ops.segment_sum(landed, recv_coarse.reshape(-1), num_segments=coarse_count)
    return (refined, coarse.astype(jnp.bfloat16))


def solution(mesh):
    placed = (
        P(("gx", "gy"), None),
        P(),
        P(),
        P(None, ("gx", "gy")),
        P(None, ("gx", "gy")),
        P(None, ("gx", "gy")),
        P(None, ("gx", "gy")),
        P(None, ("gx", "gy")),
    )
    return jax.shard_map(
        on_device,
        mesh=mesh,
        in_specs=placed,
        out_specs=(P(("gx", "gy"), None), P(("gx", "gy"), None)),
        check_vma=False,
    )
```

profile of v0, /device:TPU:14, one launch (start us, length us, event | category | flops | bytes accessed | tf_op | source)
XLA Modules:
  0.0 741.5 jit_solution(2144717783599658786)
XLA Ops:
  5.5 3.8 collective-permute-start.1
  11.1 6.1 collective-permute-start
  22.3 3.3 collective-permute-done.1
  38.1 3.3 collective-permute-done.2
  42.8 3.4 collective-permute-done.3
  47.6 6.4 stack.11
  54.0 4.5 reshape.174
  58.5 17.9 %maximum_maximum_fusion = bf16[16512,64]{1,0:T(8,128)(2,1)} fusion(bf16[8192,64]{1,0:T(8,128)(2,1)} %reshape.174, bf16[8192,64]{1,0:T(8,128)(2,1)S(1)} %copy.37, bf16[16512]{0:T(1024)(128)(2,1)S(1)} %pad.5.clone), kind=kLoop, calls=%fused_computation.27 | loop fusion | flops 6340608 | bytes 4243712 | tf_op jit(solution)/shard_map/concatenate | solution.py:64
  76.4 96.8 %while.22 = (s32[]{:T(128)}, bf16[4,16,128,64]{2,3,1,0:T(8,128)(2,1)}, s32[4,27,16]{1,2,0:T(8,128)S(1)}, bf16[129,128,64]{2,1,0:T(8,128)(2,1)}, bf16[27,64,64]{1,2,0:T(8,128)(2,1)S(1)}) while((s32[]{:T(128)}, bf16[4,16,128,64]{2,3,1,0:T(8,128)(2,1)}, s32[4,27,16]{1,2,0:T(8,128)S(1)}, bf16[129,128,64]{2,1,0:T(8,128)(2,1)}, ...), condition=%wide.region_1.2_spmd.clone, body=%wide.region_0.1_spmd.sunk.clone | while | flops 452987168 | bytes 30610436 | solution.py:78
  76.6 15.2 %gather_fusion = bf16[432,128,64]{2,1,0:T(8,128)(2,1)} fusion(bf16[129,128,64]{2,1,0:T(8,128)(2,1)} %get-tuple-element.237, s32[1024]{0:T(1024)S(1)} %pad_clamp_fusion.4), kind=kCustom, calls=%fused_computation.clone.1.clone | custom fusion | bytes 14157504 | tf_op jit(solution)/shard_map/while/body/eval_jaxpr/gather | solution.py:18
  91.8 7.8 %fusion.39 = bf16[4,16,128,64]{2,3,1,0:T(8,128)(2,1)S(1)} fusion(bf16[4,16,128,64]{2,3,1,0:T(8,128)(2,1)S(1)} %copy-done.2, s32[]{:T(128)S(6)} %copy.60, bf16[27,16,128,64]{3,2,1,0:T(8,128)(2,1)} %bitcast.86, bf16[27,64,64]{1,2,0:T(8,128)(2,1)S(1)} %get-tuple-element.238), kind=kOutput, calls=%fused_computation.6.clone.1.clone | convolution fusion | flops 452984832 | bytes 8044548 | tf_op jit(solution)/shard_map/while/body/eval_jaxpr/kgbc,kcd->gbd/dot_general | solution.py:19
  100.8 15.2 %gather_fusion = bf16[432,128,64]{2,1,0:T(8,128)(2,1)} fusion(bf16[129,128,64]{2,1,0:T(8,128)(2,1)} %get-tuple-element.237, s32[1024]{0:T(1024)S(1)} %pad_clamp_fusion.4), kind=kCustom, calls=%fused_computation.clone.1.clone | custom fusion | bytes 14157504 | tf_op jit(solution)/shard_map/while/body/eval_jaxpr/gather | solution.py:18
  116.0 7.8 %fusion.39 = bf16[4,16,128,64]{2,3,1,0:T(8,128)(2,1)S(1)} fusion(bf16[4,16,128,64]{2,3,1,0:T(8,128)(2,1)S(1)} %copy-done.2, s32[]{:T(128)S(6)} %copy.60, bf16[27,16,128,64]{3,2,1,0:T(8,128)(2,1)} %bitcast.86, bf16[27,64,64]{1,2,0:T(8,128)(2,1)S(1)} %get-tuple-element.238), kind=kOutput, calls=%fused_computation.6.clone.1.clone | convolution fusion | flops 452984832 | bytes 8044548 | tf_op jit(solution)/shard_map/while/body/eval_jaxpr/kgbc,kcd->gbd/dot_general | solution.py:19
  125.0 15.2 %gather_fusion = bf16[432,128,64]{2,1,0:T(8,128)(2,1)} fusion(bf16[129,128,64]{2,1,0:T(8,128)(2,1)} %get-tuple-element.237, s32[1024]{0:T(1024)S(1)} %pad_clamp_fusion.4), kind=kCustom, calls=%fused_computation.clone.1.clone | custom fusion | bytes 14157504 | tf_op jit(solution)/shard_map/while/body/eval_jaxpr/gather | solution.py:18
  140.2 7.8 %fusion.39 = bf16[4,16,128,64]{2,3,1,0:T(8,128)(2,1)S(1)} fusion(bf16[4,16,128,64]{2,3,1,0:T(8,128)(2,1)S(1)} %copy-done.2, s32[]{:T(128)S(6)} %copy.60, bf16[27,16,128,64]{3,2,1,0:T(8,128)(2,1)} %bitcast.86, bf16[27,64,64]{1,2,0:T(8,128)(2,1)S(1)} %get-tuple-element.238), kind=kOutput, calls=%fused_computation.6.clone.1.clone | convolution fusion | flops 452984832 | bytes 8044548 | tf_op jit(solution)/shard_map/while/body/eval_jaxpr/kgbc,kcd->gbd/dot_general | solution.py:19
  149.2 15.2 %gather_fusion = bf16[432,128,64]{2,1,0:T(8,128)(2,1)} fusion(bf16[129,128,64]{2,1,0:T(8,128)(2,1)} %get-tuple-element.237, s32[1024]{0:T(1024)S(1)} %pad_clamp_fusion.4), kind=kCustom, calls=%fused_computation.clone.1.clone | custom fusion | bytes 14157504 | tf_op jit(solution)/shard_map/while/body/eval_jaxpr/gather | solution.py:18
  164.4 7.8 %fusion.39 = bf16[4,16,128,64]{2,3,1,0:T(8,128)(2,1)S(1)} fusion(bf16[4,16,128,64]{2,3,1,0:T(8,128)(2,1)S(1)} %copy-done.2, s32[]{:T(128)S(6)} %copy.60, bf16[27,16,128,64]{3,2,1,0:T(8,128)(2,1)} %bitcast.86, bf16[27,64,64]{1,2,0:T(8,128)(2,1)S(1)} %get-tuple-element.238), kind=kOutput, calls=%fused_computation.6.clone.1.clone | convolution fusion | flops 452984832 | bytes 8044548 | tf_op jit(solution)/shard_map/while/body/eval_jaxpr/kgbc,kcd->gbd/dot_general | solution.py:19
  178.3 57.8 %gather_fusion.3 = bf16[16384,64]{1,0:T(8,128)(2,1)} fusion(bf16[8193,64]{1,0:T(8,128)(2,1)S(1)} %concatenate.7, s32[16384]{0:T(1024)S(1)} %broadcast_clamp_fusion), kind=kCustom, calls=%fused_computation.3 | custom fusion | bytes 4259840 | tf_op jit(solution)/shard_map/gather | solution.py:84
  236.2 4.8 copy.41
  241.0 217.6 %while.23 = (s32[]{:T(128)}, f32[32,512,128]{2,1,0:T(8,128)}, s32[32,512]{1,0:T(8,128)}, bf16[32,512,64]{1,2,0:T(8,128)(2,1)}, bf16[8,64,128]{2,1,0:T(8,128)(2,1)S(1)}) while((s32[]{:T(128)}, f32[32,512,128]{2,1,0:T(8,128)}, s32[32,512]{1,0:T(8,128)}, bf16[32,512,64]{1,2,0:T(8,128)(2,1)}, bf16[8,64,128]{2,1,0:T(8,128)(2,1)S(1)}) %tuple.71), condition=%wide.region_3.4_spmd.clone, body=%wide.region_2.3_spmd.sunk.clone | while | flops 67182592 | bytes 7566417 | solution.py:35
  244.3 2.6 gather_fusion.1
  251.1 2.6 gather_fusion.1
  257.9 2.6 gather_fusion.1
  264.7 2.6 gather_fusion.1
  271.5 2.6 gather_fusion.1
  278.3 2.6 gather_fusion.1
  285.1 2.6 gather_fusion.1
  291.9 2.6 gather_fusion.1
  298.7 2.6 gather_fusion.1
  305.5 2.6 gather_fusion.1
  312.3 2.6 gather_fusion.1
  319.1 2.6 gather_fusion.1
  325.8 2.6 gather_fusion.1
  332.6 2.6 gather_fusion.1
  339.4 2.6 gather_fusion.1
  346.2 2.6 gather_fusion.1
  353.0 2.6 gather_fusion.1
  359.8 2.6 gather_fusion.1
  366.6 2.6 gather_fusion.1
  373.4 2.6 gather_fusion.1
  380.2 2.6 gather_fusion.1
  387.0 2.6 gather_fusion.1
  393.8 2.6 gather_fusion.1
  400.6 2.6 gather_fusion.1
  407.4 2.6 gather_fusion.1
  458.6 9.7 %all-to-all-start = ((f32[32,512,128]{2,1,0:T(8,128)}), f32[32,512,128]{2,1,0:T(8,128)}, u32[]{:S(2)}, u32[]{:S(2)}) async-start(f32[32,512,128]{2,1,0:T(8,128)} %get-tuple-element.57), calls=%async_computation | async-start | bytes 16777216 | tf_op jit(solution)/shard_map/all_to_all | solution.py:90
  469.9 182.8 %all-to-all-done = f32[32,512,128]{2,1,0:T(8,128)} async-done(((f32[32,512,128]{2,1,0:T(8,128)}), f32[32,512,128]{2,1,0:T(8,128)}, u32[]{:S(2)}, u32[]{:S(2)}) %all-to-all-start) | async-done | bytes 8388640 | tf_op jit(solution)/shard_map/all_to_all | solution.py:90
  652.7 87.9 %scatter_custom_fusion = f32[2048,128]{1,0:T(8,128)S(1)} fusion(s32[16384]{0:T(1024)S(1)} %bitcast.98, f32[16384,128]{1,0:T(8,128)} %bitcast.19, f32[]{:T(128)} %constant.31.clone.1), kind=kCustom, calls=%fused_computation.32 | custom fusion | flops 2097152 | bytes 1049088 | tf_op jit(solution)/shard_map/scatter-add | solution.py:93
  (351 shorter events, 189.5 us)
Async XLA Ops:
  3.8 15.6 %copy-start.7 = (s32[27,64]{1,0:T(8,128)S(1)}, s32[27,64]{1,0:T(8,128)}, u32[]{:S(2)}) copy-start(s32[27,64]{1,0:T(8,128)} %param.15) | copy-start | bytes 20740
  5.5 20.1 %collective-permute-start.1 = (bf16[3,65536]{1,0:T(4,128)(2,1)}, bf16[3,65536]{1,0:T(4,128)(2,1)S(1)}, u32[]{:S(2)}, u32[]{:S(2)}) collective-permute-start(bf16[3,65536]{1,0:T(4,128)(2,1)} %slice.70), channel_id=1, source_target_pairs={{0,8},{8,16},{16,24},{24,32},{32,40},{40,48},{48,56},{56,64},{64,7... | collective-permute-start | bytes 1179656 | tf_op jit(solution)/shard_map/ppermute | solution.py:14
  9.4 12.8 %copy-start.5 = (s32[32,512]{1,0:T(8,128)S(1)}, s32[32,512]{1,0:T(8,128)}, u32[]{:S(2)}) copy-start(s32[32,512]{1,0:T(8,128)} %param.17) | copy-start | bytes 196612
  11.1 17.6 %collective-permute-start = (bf16[3,65536]{1,0:T(4,128)(2,1)}, bf16[3,65536]{1,0:T(4,128)(2,1)}, u32[]{:S(2)}, u32[]{:S(2)}) collective-permute-start(bf16[3,65536]{1,0:T(4,128)(2,1)} %slice.65), channel_id=1, source_target_pairs={{8,0},{16,8},{24,16},{32,24},{40,32},{48,40},{56,48},{64,56},{72,6... | collective-permute-start | bytes 1179656 | tf_op jit(solution)/shard_map/ppermute | solution.py:14
  26.9 20.7 %copy-start.4 = (bf16[1,65536]{1,0:T(2,128)(2,1)S(1)}, bf16[1,65536]{1,0:T(2,128)(2,1)}, u32[]{:S(2)}) copy-start(bf16[1,65536]{1,0:T(2,128)(2,1)} %get-tuple-element.123) | copy-start | bytes 393220
  32.8 8.6 %collective-permute-start.2 = (bf16[3,65536]{1,0:T(4,128)(2,1)S(1)}, bf16[3,65536]{1,0:T(4,128)(2,1)S(1)}, u32[]{:S(2)}, u32[]{:S(2)}) collective-permute-start(bf16[3,65536]{1,0:T(4,128)(2,1)S(1)} %pad_maximum_fusion), channel_id=1, source_target_pairs={{1,0},{2,1},{3,2},{4,3},{5,4},{6,5},{7,6},{9,8},{10,9},{11,10},{12... | collective-permute-start | bytes 1179656 | tf_op jit(solution)/shard_map/ppermute | solution.py:14
  35.7 10.5 %collective-permute-start.3 = (bf16[3,65536]{1,0:T(4,128)(2,1)S(1)}, bf16[3,65536]{1,0:T(4,128)(2,1)S(1)}, u32[]{:S(2)}, u32[]{:S(2)}) collective-permute-start(bf16[3,65536]{1,0:T(4,128)(2,1)S(1)} %pad_maximum_fusion.1), channel_id=1, source_target_pairs={{0,1},{1,2},{2,3},{3,4},{4,5},{5,6},{6,7},{8,9},{9,10},{10,11},{11... | collective-permute-start | bytes 1179656 | tf_op jit(solution)/shard_map/ppermute | solution.py:14
  76.6 15.2 %copy-start.2 = (bf16[4,16,128,64]{2,3,1,0:T(8,128)(2,1)S(1)}, bf16[4,16,128,64]{2,3,1,0:T(8,128)(2,1)}, u32[]{:S(2)}) copy-start(bf16[4,16,128,64]{2,3,1,0:T(8,128)(2,1)} %get-tuple-element.230) | copy-start | bytes 3145732 | tf_op jit(solution)/shard_map/while
  99.6 1.0 copy-start.3
  100.8 15.2 %copy-start.2 = (bf16[4,16,128,64]{2,3,1,0:T(8,128)(2,1)S(1)}, bf16[4,16,128,64]{2,3,1,0:T(8,128)(2,1)}, u32[]{:S(2)}) copy-start(bf16[4,16,128,64]{2,3,1,0:T(8,128)(2,1)} %get-tuple-element.230) | copy-start | bytes 3145732 | tf_op jit(solution)/shard_map/while
  123.9 1.0 copy-start.3
  125.0 15.2 %copy-start.2 = (bf16[4,16,128,64]{2,3,1,0:T(8,128)(2,1)S(1)}, bf16[4,16,128,64]{2,3,1,0:T(8,128)(2,1)}, u32[]{:S(2)}) copy-start(bf16[4,16,128,64]{2,3,1,0:T(8,128)(2,1)} %get-tuple-element.230) | copy-start | bytes 3145732 | tf_op jit(solution)/shard_map/while
  148.1 1.0 copy-start.3
  149.2 15.2 %copy-start.2 = (bf16[4,16,128,64]{2,3,1,0:T(8,128)(2,1)S(1)}, bf16[4,16,128,64]{2,3,1,0:T(8,128)(2,1)}, u32[]{:S(2)}) copy-start(bf16[4,16,128,64]{2,3,1,0:T(8,128)(2,1)} %get-tuple-element.230) | copy-start | bytes 3145732 | tf_op jit(solution)/shard_map/while
  172.2 1.0 copy-start.3
  236.2 4.8 copy-start.1
  458.6 9.7 %copy-start.6 = (s32[32,512]{1,0:T(8,128)S(1)}, s32[32,512]{1,0:T(8,128)}, u32[]{:S(2)}) copy-start(s32[32,512]{1,0:T(8,128)} %param.19) | copy-start | bytes 196612
  458.6 9.7 %copy-start = (bf16[4,16,128,64]{3,2,1,0:T(8,128)(2,1)S(1)}, bf16[4,16,128,64]{3,2,1,0:T(8,128)(2,1)}, u32[]{:S(2)}) copy-start(bf16[4,16,128,64]{3,2,1,0:T(8,128)(2,1)} %copy.40) | copy-start | bytes 3145732
  458.6 194.2 %all-to-all-start = ((f32[32,512,128]{2,1,0:T(8,128)}), f32[32,512,128]{2,1,0:T(8,128)}, u32[]{:S(2)}, u32[]{:S(2)}) async-start(f32[32,512,128]{2,1,0:T(8,128)} %get-tuple-element.57), calls=%async_computation | async-start | bytes 16777216 | tf_op jit(solution)/shard_map/all_to_all | solution.py:90
where the time goes:
time: 748 us; the launch traced here: 741 us
  local copies, waits for them, and re-layouts  285 us (38%)
  waiting for transfers between devices  195 us (26%)
  other arithmetic  163 us (22%)
  matrix products  72.6 us (10%)
  starting transfers between devices  23.9 us (3%)
    all_to_all x1, waiting for transfers between devices, on_device(): lax.all_to_all(contributions, 'gx', split_axis=0, concat_axis=0, tiled=True)  183 us
    scatter-add x1, other arithmetic, on_device(): jax.ops.segment_sum(landed, recv_coarse.reshape(-1), num_segments=coarse_...  87.9 us
    gather x32, local copies, waits for them, and re-layouts, product_group(): jnp.take_along_axis(every_sub, group_codes[:, None, None], axis=1)[:, 0]  84.5 us
    gather x4, local copies, waits for them, and re-layouts, block_convolve_step(): picked = table_blocks[offsets]  60.8 us
    gather x1, local copies, waits for them, and re-layouts, on_device(): slot_rows = padded_fine[send_rows.reshape(-1)]  57.8 us
    dot_general x32, matrix products, product_group(): jnp.einsum('rc,scd->rsd', group_rows, weights, preferred_element_type=jnp...  41.3 us
    dot_general x32, local copies, waits for them, and re-layouts, product_group(): jnp.einsum('rc,scd->rsd', group_rows, weights, preferred_element_type=jnp...  39 us
    dot_general x4, matrix products, block_convolve_step(): jnp.einsum('kgbc,kcd->gbd', picked, weights, preferred_element_type=jnp.f...  31.3 us
  transfers between devices with their start and end apart: 5, of which 5 were waited for; matrix products, arithmetic and copies ran while one was open for 2% of the time, Pallas kernels for 0%

commit v1 on v0

v1 whole, which is shorter than its diff:
```python
import functools

import jax
import jax.numpy as jnp
from jax import lax
from jax.experimental import pallas as pl
from jax.experimental.pallas import tpu as pltpu
from jax.sharding import PartitionSpec as P

MESH = pl.DeviceIdType.MESH
BLOCK = 128
DIRECTIONS = ((-1, -1), (-1, 0), (-1, 1), (0, -1), (0, 1), (1, -1), (1, 0), (1, 1))
VMEM_LIMIT = 60 * 1024 * 1024


def pack_kernel(halo_ref, feat_ref, out_ref):
    channels = feat_ref.shape[0]
    directions, per_direction = halo_ref.shape

    @pl.loop(0, directions)
    def _(j):
        for m in range(per_direction):
            column = pl.multiple_of(halo_ref[j, m] * BLOCK, BLOCK)
            out_ref[j, m * channels : (m + 1) * channels, :] = feat_ref[:, pl.ds(column, BLOCK)]


def halo_kernel(n_gx, n_gy, sent, out_ref, send_sem, recv_sem):
    gx, gy = lax.axis_index("gx"), lax.axis_index("gy")
    barrier = pltpu.get_barrier_semaphore()
    for dx, dy in DIRECTIONS:
        peer = (lax.rem(gx + dx + n_gx, n_gx), lax.rem(gy + dy + n_gy, n_gy))
        pl.semaphore_signal(barrier, inc=1, device_id=peer, device_id_type=MESH)
    pl.semaphore_wait(barrier, len(DIRECTIONS))

    def inside(x, y):
        return (x >= 0) & (x < n_gx) & (y >= 0) & (y < n_gy)

    def copy(j, peer):
        return pltpu.make_async_remote_copy(
            src_ref=sent.at[j],
            dst_ref=out_ref.at[j],
            send_sem=send_sem.at[j],
            recv_sem=recv_sem.at[j],
            device_id=peer,
            device_id_type=MESH,
        )

    for j, (dx, dy) in enumerate(DIRECTIONS):
        @pl.when(inside(gx + dx, gy + dy))
        def _():
            copy(j, (gx + dx, gy + dy)).start()

    for j, (dx, dy) in enumerate(DIRECTIONS):
        @pl.when(jnp.logical_not(inside(gx - dx, gy - dy)))
        def _():
            out_ref[j] = jnp.zeros(out_ref.shape[1:], out_ref.dtype)

    for j, (dx, dy) in enumerate(DIRECTIONS):
        @pl.when(inside(gx - dx, gy - dy))
        def _():
            copy(j, (gx, gy)).wait_recv()

        @pl.when(inside(gx + dx, gy + dy))
        def _():
            copy(j, (gx, gy)).wait_send()


def exchange_halo(feat_t, halo_rows, n_gx, n_gy):
    channels = feat_t.shape[0]
    directions, per_direction = halo_rows.shape
    page = (directions, per_direction * channels, BLOCK)
    vmem = pl.BlockSpec(memory_space=pltpu.VMEM)
    sent = pl.pallas_call(
        pack_kernel,
        out_shape=jax.ShapeDtypeStruct(page, feat_t.dtype),
        in_specs=[pl.BlockSpec(memory_space=pltpu.SMEM), vmem],
        out_specs=vmem,
        name="pack",
    )(halo_rows, feat_t)
    return pl.pallas_call(
        functools.partial(halo_kernel, n_gx, n_gy),
        out_shape=jax.ShapeDtypeStruct(page, feat_t.dtype),
        in_specs=[vmem],
        out_specs=vmem,
        scratch_shapes=[
            pltpu.SemaphoreType.DMA((directions,)),
            pltpu.SemaphoreType.DMA((directions,)),
        ],
        compiler_params=pltpu.CompilerParams(collective_id=0, has_side_effects=True),
        name="halo",
    )(sent)


def doubled_rows(block):
    wide = jnp.concatenate([block, block], axis=0)
    return jnp.transpose(wide)


def conv_kernel(
    group, map_ref, rows_ref, feat_ref, halo_ref, w_ref, out_ref, slot_ref,
    table, weights, lhs, fine, stage,
):
    offsets, blocks = map_ref.shape
    channels, voxels = feat_ref.shape
    halo_blocks = halo_ref.shape[0] // channels
    peers, half, lanes = slot_ref.shape
    pairs = (offsets + 1) // 2
    low = lax.broadcasted_iota(jnp.int32, (BLOCK, lanes), 1) < channels

    weights[...] = jnp.zeros(weights.shape, weights.dtype)
    weights[: offsets * channels, :] = jnp.concatenate([w_ref[...], w_ref[...]], axis=1)

    @pl.loop(0, blocks)
    def _(i):
        column = pl.multiple_of(i * BLOCK, BLOCK)
        table[pl.ds(column, BLOCK), :] = doubled_rows(feat_ref[:, pl.ds(column, BLOCK)])

    @pl.loop(0, halo_blocks)
    def _(i):
        row = pl.multiple_of((blocks + i) * BLOCK, BLOCK)
        source = pl.multiple_of(i * channels, channels)
        table[pl.ds(row, BLOCK), :] = doubled_rows(halo_ref[pl.ds(source, channels), :])

    empty = (blocks + halo_blocks) * BLOCK
    table[empty : empty + BLOCK, :] = jnp.zeros((BLOCK, lanes), table.dtype)
    fine[voxels : voxels + 8, :] = jnp.zeros((8, lanes), fine.dtype)

    def pick(k, i):
        return table[pl.ds(pl.multiple_of(map_ref[k, i] * BLOCK, BLOCK), BLOCK), :]

    @pl.loop(0, blocks // group)
    def _(g):
        for b in range(group):
            i = g * group + b
            for pair in range(pairs):
                first = pick(2 * pair, i)
                if 2 * pair + 1 < offsets:
                    both = jnp.where(low, first, pick(2 * pair + 1, i))
                else:
                    both = jnp.where(low, first, jnp.zeros_like(first))
                lhs[b * BLOCK : (b + 1) * BLOCK, pair * lanes : (pair + 1) * lanes] = both
        total = jnp.dot(lhs[...], weights[...], preferred_element_type=jnp.float32)
        refined = jnp.maximum(total, 0.0).astype(jnp.bfloat16).astype(jnp.float32)
        start = pl.multiple_of(g * group * BLOCK, group * BLOCK)
        fine[pl.ds(start, group * BLOCK), :] = refined
        for b in range(group):
            block = refined[b * BLOCK : (b + 1) * BLOCK, :]
            column = pl.multiple_of(start + b * BLOCK, BLOCK)
            out_ref[:, pl.ds(column, BLOCK)] = jnp.transpose(block)[:channels, :].astype(
                out_ref.dtype
            )

    low_row = lax.broadcasted_iota(jnp.int32, (1, lanes), 1) < channels

    @pl.loop(0, peers)
    def _(p):
        for c in range(half):
            first = fine[pl.ds(rows_ref[p, c], 1), :]
            second = fine[pl.ds(rows_ref[p, half + c], 1), :]
            stage[c : c + 1, :] = jnp.where(low_row, first, second)
        slot_ref[p] = stage[...].astype(slot_ref.dtype)


def convolve(feat_t, halo, conv_weight, kernel_map, send_rows):
    channels, voxels = feat_t.shape
    offsets, blocks = kernel_map.shape
    peers, capacity = send_rows.shape
    group = 8
    pairs = (offsets + 1) // 2
    lanes = 2 * channels
    halo_blocks = halo.shape[0] // channels
    vmem = pl.BlockSpec(memory_space=pltpu.VMEM)
    smem = pl.BlockSpec(memory_space=pltpu.SMEM)
    return pl.pallas_call(
        functools.partial(conv_kernel, group),
        out_shape=(
            jax.ShapeDtypeStruct((channels, voxels), jnp.bfloat16),
            jax.ShapeDtypeStruct((peers, capacity // 2, lanes), jnp.bfloat16),
        ),
        in_specs=[smem, smem, vmem, vmem, vmem],
        out_specs=(vmem, vmem),
        scratch_shapes=[
            pltpu.VMEM(((blocks + halo_blocks + 1) * BLOCK, lanes), jnp.bfloat16),
            pltpu.VMEM((pairs * lanes, lanes), jnp.bfloat16),
            pltpu.VMEM((group * BLOCK, pairs * lanes), jnp.bfloat16),
            pltpu.VMEM((voxels + 8, lanes), jnp.float32),
            pltpu.VMEM((capacity // 2, lanes), jnp.float32),
        ],
        compiler_params=pltpu.CompilerParams(vmem_limit_bytes=VMEM_LIMIT),
        name="convolve",
    )(kernel_map, send_rows, feat_t, halo, conv_weight.reshape(offsets * channels, channels))


def reduce_kernel(slot_ref, sub_ref, coarse_ref, w_ref, out_ref, wide, placed, terms, hot, total):
    peers, half, lanes = slot_ref.shape
    subs, channels, width = w_ref.shape
    coarse_count = out_ref.shape[0]
    wide[...] = jnp.zeros(wide.shape, wide.dtype)
    for s in range(subs):
        wide[s * lanes : s * lanes + channels, :width] = w_ref[s]
        wide[s * lanes + channels : (s + 1) * lanes, width:] = w_ref[s]
    total[...] = jnp.zeros(total.shape, total.dtype)
    ids = lax.broadcasted_iota(jnp.int32, (BLOCK, 2 * half), 0).astype(jnp.bfloat16)

    @pl.loop(0, peers)
    def _(a):
        code = sub_ref[pl.ds(a, 1), :].astype(jnp.float32)
        spread = jnp.concatenate(
            [
                jnp.broadcast_to(code[:, :half], (channels, half)),
                jnp.broadcast_to(code[:, half:], (channels, half)),
            ],
            axis=0,
        )
        column = jnp.transpose(spread).astype(jnp.bfloat16)
        rows = slot_ref[a]
        for s in range(subs):
            placed[:, s * lanes : (s + 1) * lanes] = jnp.where(
                column == jnp.bfloat16(s), rows, jnp.zeros_like(rows)
            )
        product = jnp.dot(placed[...], wide[...], preferred_element_type=jnp.float32)
        high = product.astype(jnp.bfloat16)
        rest = (product - high.astype(jnp.float32)).astype(jnp.bfloat16)
        terms[:half, :width] = high[:, :width]
        terms[:half, width:] = rest[:, :width]
        terms[half:, :width] = high[:, width:]
        terms[half:, width:] = rest[:, width:]
        target = coarse_ref[pl.ds(a, 1), :]
        upper = target // BLOCK
        lower = target - upper * BLOCK
        for h in range(coarse_count // BLOCK):
            wanted = jnp.where(upper == h, lower, -1).astype(jnp.float32).astype(jnp.bfloat16)
            hot[h * BLOCK : (h + 1) * BLOCK, :] = jnp.where(
                ids == wanted, jnp.bfloat16(1), jnp.bfloat16(0)
            )
        total[...] += jnp.dot(hot[...], terms[...], preferred_element_type=jnp.float32)

    out_ref[...] = (total[:, :width] + total[:, width:]).astype(out_ref.dtype)


def reduce_coarse(slots, subs, recv_coarse, down_weight, coarse_count):
    peers, half, lanes = slots.shape
    width = down_weight.shape[2]
    vmem = pl.BlockSpec(memory_space=pltpu.VMEM)
    return pl.pallas_call(
        reduce_kernel,
        out_shape=jax.ShapeDtypeStruct((coarse_count, width), jnp.bfloat16),
        in_specs=[vmem] * 4,
        out_specs=vmem,
        scratch_shapes=[
            pltpu.VMEM((down_weight.shape[0] * lanes, 2 * width), jnp.bfloat16),
            pltpu.VMEM((half, down_weight.shape[0] * lanes), jnp.bfloat16),
            pltpu.VMEM((2 * half, 2 * width), jnp.bfloat16),
            pltpu.VMEM((coarse_count, 2 * half), jnp.bfloat16),
            pltpu.VMEM((coarse_count, 2 * width), jnp.float32),
        ],
        compiler_params=pltpu.CompilerParams(vmem_limit_bytes=VMEM_LIMIT),
        name="reduce",
    )(slots, subs, recv_coarse, down_weight)


def on_device(
    n_gx, n_gy,
    features, conv_weight, down_weight, kernel_map, halo_rows, send_rows, send_sub, recv_coarse,
):
    voxels, channels = features.shape
    subs = lax.all_to_all(send_sub, "gx", split_axis=0, concat_axis=0, tiled=True)
    feat_t = features.T
    halo = exchange_halo(feat_t, halo_rows, n_gx, n_gy).reshape(-1, BLOCK)
    refined_t, slots = convolve(feat_t, halo, conv_weight, kernel_map, send_rows)
    landed = lax.all_to_all(slots, "gx", split_axis=0, concat_axis=0, tiled=True)
    coarse = reduce_coarse(landed, subs, recv_coarse, down_weight, voxels // 4)
    return refined_t.T, coarse


def solution(mesh):
    split = P(None, ("gx", "gy"))
    return jax.shard_map(
        functools.partial(on_device, mesh.shape["gx"], mesh.shape["gy"]),
        mesh=mesh,
        in_specs=(P(("gx", "gy"), None), P(), P(), split, split, split, split, split),
        out_specs=(P(("gx", "gy"), None), P(("gx", "gy"), None)),
        check_vma=False,
    )
```

time: 748 us -> 182 us (0.24)
  local copies, waits for them, and re-layouts: 285 us -> 3.48 us
  other arithmetic: 163 us -> 0 us
  waiting for transfers between devices: 195 us -> 48.5 us
  Pallas kernels: 0 us -> 107 us
  matrix products: 72.6 us -> 0 us
    gather x38 -> x0, local copies, waits for them, and re-layouts: 204 us -> none  [the longest x32 84.5 us: product_group(): jnp.take_along_axis(every_sub, group_codes[:, None, None], axis=1)[:, 0]]
    all_to_all x1 -> x2, waiting for transfers between devices: 183 us -> 48.5 us  [the longest x1 48.5 us: on_device(): lax.all_to_all(slots, 'gx', split_axis=0, concat_axis=0, tiled=True)]
    pallas_call x0 -> x4, Pallas kernels: none -> 107 us  [the longest x1 45.5 us: reduce_coarse(): pl.pallas_call(reduce_kernel, out_shape=jax.ShapeDtypeStruct((coarse_coun...]
    scatter-add x1 -> x0, other arithmetic: 87.9 us -> none  [on_device(): jax.ops.segment_sum(landed, recv_coarse.reshape(-1), num_segments=coarse_...]
    dot_general x36 -> x0, matrix products: 72.6 us -> none  [the longest x32 41.3 us: product_group(): jnp.einsum('rc,scd->rsd', group_rows, weights, preferred_element_type=jnp...]
    dot_general x32 -> x0, local copies, waits for them, and re-layouts: 39 us -> none  [product_group(): jnp.einsum('rc,scd->rsd', group_rows, weights, preferred_element_type=jnp...]
    dynamic_update_slice x32 -> x0, other arithmetic: 27.1 us -> none  [sub_products(): result = lax.map(product_group, (grouped_rows, grouped_codes))]
    select_n x38 -> x0, other arithmetic: 24.2 us -> none  [the longest x32 23.4 us: product_group(): jnp.take_along_axis(every_sub, group_codes[:, None, None], axis=1)[:, 0]]
  transfers between devices with their start and end apart: 5 -> 2, of which waited for: 5 -> 1; matrix products, arithmetic and copies ran while one was open for 2% -> 0% of each run, Pallas kernels for 0% -> 34%
where the time goes in v1:
time: 182 us; the launch traced here: 180 us
  Pallas kernels  107 us (59%)
  waiting for transfers between devices  48.5 us (27%)
  starting transfers between devices  20.2 us (11%)
  local copies, waits for them, and re-layouts  3.48 us (2%)
    all_to_all x1, waiting for transfers between devices, on_device(): lax.all_to_all(slots, 'gx', split_axis=0, concat_axis=0, tiled=True)  48.5 us
    pallas_call x1, Pallas kernels, reduce_coarse(): pl.pallas_call(reduce_kernel, out_shape=jax.ShapeDtypeStruct((coarse_coun...  45.5 us
    pallas_call x1, Pallas kernels, convolve(): pl.pallas_call(functools.partial(conv_kernel, group), out_shape=(jax.Shap...  43.7 us
    pallas_call x1, Pallas kernels, exchange_halo(): pl.pallas_call(functools.partial(halo_kernel, n_gx, n_gy), out_shape=jax....  15.7 us
    all_to_all x1, starting transfers between devices, on_device(): lax.all_to_all(send_sub, 'gx', split_axis=0, concat_axis=0, tiled=True)  11.6 us
    all_to_all x1, starting transfers between devices, on_device(): lax.all_to_all(slots, 'gx', split_axis=0, concat_axis=0, tiled=True)  8.61 us
  transfers between devices with their start and end apart: 2, of which 1 were waited for; matrix products, arithmetic and copies ran while one was open for 0% of the time, Pallas kernels for 34%

profile of v1, /device:TPU:14, one launch (start us, length us, event | category | flops | bytes accessed | tf_op | source)
XLA Modules:
  0.0 180.2 jit_solution(9433847245780583800)
XLA Ops:
  0.6 1.5 all_to_all.11
  2.1 11.6 %all-to-all-start.1 = ((s32[32,1,512]{2,1,0:T(1,128)}), s32[32,1,512]{2,1,0:T(1,128)S(1)}, u32[]{:S(2)}, u32[]{:S(2)}) async-start(s32[32,1,512]{2,1,0:T(1,128)} %all_to_all.11), calls=%async_computation.1 | async-start | bytes 131072 | tf_op jit(solution)/shard_map/all_to_all | solution.py:267
  13.8 2.5 %pack.1.sent = bf16[8,512,128]{2,1,0:T(8,128)(2,1)} custom-call(s32[8,8]{1,0:T(8,128)} %halo_ref.1, bf16[64,8192]{1,0:T(8,128)(2,1)} %bitcast.7), custom_call_target="tpu_custom_call" | custom-call | tf_op jit(solution)/shard_map/pack/pallas_call | solution.py:73
  16.3 15.7 %halo.1 = bf16[8,512,128]{2,1,0:T(8,128)(2,1)} custom-call(bf16[8,512,128]{2,1,0:T(8,128)(2,1)} %pack.1.sent), custom_call_target="tpu_custom_call" | custom-call | tf_op jit(solution)/shard_map/halo/pallas_call | solution.py:80
  31.9 43.7 %convolve.1 = (bf16[64,8192]{1,0:T(8,128)(2,1)}, bf16[32,256,128]{2,1,0:T(8,128)(2,1)}) custom-call(s32[27,64]{1,0:T(8,128)} %map_ref.1, s32[32,512]{1,0:T(8,128)} %rows_ref.1, bf16[64,8192]{1,0:T(8,128)(2,1)} %bitcast.8, bf16[4096,128]{1,0:T(8,128)(2,1)} %bitcast.9, bf16[1728,64]{1,0:T(8,128)(2,1)} %bitcast.10), custom_call_target="tpu_custom_call" | custom-call | tf_op jit(solution)/shard_map/convolve/pallas_call | solution.py:174
  75.7 0.0 all-to-all-done.1
  75.7 8.6 %all-to-all-start = ((bf16[32,256,128]{2,1,0:T(8,128)(2,1)}), bf16[32,256,128]{2,1,0:T(8,128)(2,1)S(1)}, u32[]{:S(2)}, u32[]{:S(2)}) async-start(bf16[32,256,128]{2,1,0:T(8,128)(2,1)} %get-tuple-element.5), calls=%async_computation | async-start | bytes 4194304 | tf_op jit(solution)/shard_map/all_to_all | solution.py:271
  84.3 0.6 copy.12
  84.9 48.5 %all-to-all-done.slot_ref = bf16[32,256,128]{2,1,0:T(8,128)(2,1)S(1)} async-done(((bf16[32,256,128]{2,1,0:T(8,128)(2,1)}), bf16[32,256,128]{2,1,0:T(8,128)(2,1)S(1)}, u32[]{:S(2)}, u32[]{:S(2)}) %all-to-all-start) | async-done | bytes 2097184 | tf_op jit(solution)/shard_map/all_to_all | solution.py:271
  133.4 0.0 copy-start
  133.4 1.3 copy-done
  134.8 45.5 %reduce.1 = bf16[2048,128]{1,0:T(8,128)(2,1)} custom-call(bf16[32,256,128]{2,1,0:T(8,128)(2,1)} %copy-done, s32[32,512]{1,0:T(8,128)} %bitcast.11, s32[32,512]{1,0:T(8,128)} %coarse_ref.1, bf16[8,64,128]{2,1,0:T(8,128)(2,1)} %w_ref.1), custom_call_target="tpu_custom_call" | custom-call | tf_op jit(solution)/shard_map/reduce/pallas_call | solution.py:245
Async XLA Ops:
  2.1 73.5 %all-to-all-start.1 = ((s32[32,1,512]{2,1,0:T(1,128)}), s32[32,1,512]{2,1,0:T(1,128)S(1)}, u32[]{:S(2)}, u32[]{:S(2)}) async-start(s32[32,1,512]{2,1,0:T(1,128)} %all_to_all.11), calls=%async_computation.1 | async-start | bytes 131072 | tf_op jit(solution)/shard_map/all_to_all | solution.py:267
  75.7 57.8 %all-to-all-start = ((bf16[32,256,128]{2,1,0:T(8,128)(2,1)}), bf16[32,256,128]{2,1,0:T(8,128)(2,1)S(1)}, u32[]{:S(2)}, u32[]{:S(2)}) async-start(bf16[32,256,128]{2,1,0:T(8,128)(2,1)} %get-tuple-element.5), calls=%async_computation | async-start | bytes 4194304 | tf_op jit(solution)/shard_map/all_to_all | solution.py:271
  133.4 1.3 copy-start

commit v2 on v1

--- a/solution.py
+++ b/solution.py
@@ -191,20 +191,78 @@
     )(kernel_map, send_rows, feat_t, halo, conv_weight.reshape(offsets * channels, channels))
 
 
-def reduce_kernel(slot_ref, sub_ref, coarse_ref, w_ref, out_ref, wide, placed, terms, hot, total):
+def torus_peer(me, depth, n_gx, step):
+    spread = lax.rem(step, depth)
+    odd = lax.rem(spread, 2)
+    ahead = odd * ((spread + 1) // 2) + (1 - odd) * (depth - spread // 2)
+    across, along = me // depth, lax.rem(me, depth)
+    wide = n_gx // depth
+    there = lax.rem(across + step // depth, wide)
+    back = lax.rem(across - step // depth + wide, wide)
+    to = there * depth + lax.rem(along + ahead, depth)
+    source = back * depth + lax.rem(along - ahead + depth, depth)
+    return to, source
+
+
+def exchange_kernel(
+    n_gx, depth, window,
+    slot_ref, sub_ref, coarse_ref, w_ref, out_ref,
+    landed, codes, wide, placed, terms, hot, total,
+    row_send, row_recv, code_send, code_recv, own_sem,
+):
+    me, gy = lax.axis_index("gx"), lax.axis_index("gy")
     peers, half, lanes = slot_ref.shape
     subs, channels, width = w_ref.shape
     coarse_count = out_ref.shape[0]
+
+    barrier = pltpu.get_barrier_semaphore()
+
+    @pl.loop(1, n_gx)
+    def _(step):
+        to, source = torus_peer(me, depth, n_gx, step)
+        pl.semaphore_signal(barrier, inc=1, device_id=(to, gy), device_id_type=MESH)
+
+    own_rows = pltpu.make_async_copy(slot_ref.at[me], landed.at[0], own_sem.at[0])
+    own_codes = pltpu.make_async_copy(sub_ref.at[me], codes.at[0], own_sem.at[1])
+    own_rows.start()
+    own_codes.start()
+
     wide[...] = jnp.zeros(wide.shape, wide.dtype)
     for s in range(subs):
         wide[s * lanes : s * lanes + channels, :width] = w_ref[s]
         wide[s * lanes + channels : (s + 1) * lanes, width:] = w_ref[s]
     total[...] = jnp.zeros(total.shape, total.dtype)
     ids = lax.broadcasted_iota(jnp.int32, (BLOCK, 2 * half), 0).astype(jnp.bfloat16)
-
-    @pl.loop(0, peers)
-    def _(a):
-        code = sub_ref[pl.ds(a, 1), :].astype(jnp.float32)
+    pl.semaphore_wait(barrier, n_gx - 1)
+
+    def rows_copy(step, to):
+        return pltpu.make_async_remote_copy(
+            src_ref=slot_ref.at[to],
+            dst_ref=landed.at[step],
+            send_sem=row_send.at[step],
+            recv_sem=row_recv.at[step],
+            device_id=(to, gy),
+            device_id_type=MESH,
+        )
+
+    def codes_copy(step, to):
+        return pltpu.make_async_remote_copy(
+            src_ref=sub_ref.at[to],
+            dst_ref=codes.at[step],
+            send_sem=code_send.at[step],
+            recv_sem=code_recv.at[step],
+            device_id=(to, gy),
+            device_id_type=MESH,
+        )
+
+    def send(step):
+        to, source = torus_peer(me, depth, n_gx, step)
+        codes_copy(step, to).start()
+        rows_copy(step, to).start()
+
+    def reduce(step):
+        to, source = torus_peer(me, depth, n_gx, step)
+        code = codes[step].astype(jnp.float32)
         spread = jnp.concatenate(
             [
                 jnp.broadcast_to(code[:, :half], (channels, half)),
@@ -213,7 +271,7 @@
             axis=0,
         )
         column = jnp.transpose(spread).astype(jnp.bfloat16)
-        rows = slot_ref[a]
+        rows = landed[step]
         for s in range(subs):
             placed[:, s * lanes : (s + 1) * lanes] = jnp.where(
                 column == jnp.bfloat16(s), rows, jnp.zeros_like(rows)
@@ -225,7 +283,7 @@
         terms[:half, width:] = rest[:, :width]
         terms[half:, :width] = high[:, width:]
         terms[half:, width:] = rest[:, width:]
-        target = coarse_ref[pl.ds(a, 1), :]
+        target = coarse_ref[pl.ds(source, 1), :]
         upper = target // BLOCK
         lower = target - upper * BLOCK
         for h in range(coarse_count // BLOCK):
@@ -235,28 +293,64 @@
             )
         total[...] += jnp.dot(hot[...], terms[...], preferred_element_type=jnp.float32)
 
+    @pl.loop(1, window)
+    def _(step):
+        send(step)
+
+    own_rows.wait()
+    own_codes.wait()
+
+    @pl.loop(0, n_gx)
+    def _(step):
+        @pl.when(step + window < n_gx)
+        def _():
+            send(step + window)
+
+        @pl.when(step > 0)
+        def _():
+            codes_copy(step, me).wait_recv()
+            rows_copy(step, me).wait_recv()
+
+        reduce(step)
+
+    @pl.loop(1, n_gx)
+    def _(step):
+        codes_copy(step, me).wait_send()
+        rows_copy(step, me).wait_send()
+
     out_ref[...] = (total[:, :width] + total[:, width:]).astype(out_ref.dtype)
 
 
-def reduce_coarse(slots, subs, recv_coarse, down_weight, coarse_count):
+def exchange_and_reduce(slots, send_sub, recv_coarse, down_weight, coarse_count, n_gx):
     peers, half, lanes = slots.shape
     width = down_weight.shape[2]
+    depth = 8
+    window = 13
     vmem = pl.BlockSpec(memory_space=pltpu.VMEM)
     return pl.pallas_call(
-        reduce_kernel,
+        functools.partial(exchange_kernel, n_gx, depth, window),
         out_shape=jax.ShapeDtypeStruct((coarse_count, width), jnp.bfloat16),
-        in_specs=[vmem] * 4,
+        in_specs=[pl.BlockSpec(memory_space=pl.ANY), vmem, vmem, vmem],
         out_specs=vmem,
         scratch_shapes=[
+            pltpu.VMEM((peers, half, lanes), jnp.bfloat16),
+            pltpu.VMEM((peers, 1, 2 * half), jnp.int32),
             pltpu.VMEM((down_weight.shape[0] * lanes, 2 * width), jnp.bfloat16),
             pltpu.VMEM((half, down_weight.shape[0] * lanes), jnp.bfloat16),
             pltpu.VMEM((2 * half, 2 * width), jnp.bfloat16),
             pltpu.VMEM((coarse_count, 2 * half), jnp.bfloat16),
             pltpu.VMEM((coarse_count, 2 * width), jnp.float32),
+            pltpu.SemaphoreType.DMA((peers,)),
+            pltpu.SemaphoreType.DMA((peers,)),
+            pltpu.SemaphoreType.DMA((peers,)),
+            pltpu.SemaphoreType.DMA((peers,)),
+            pltpu.SemaphoreType.DMA((2,)),
         ],
-        compiler_params=pltpu.CompilerParams(vmem_limit_bytes=VMEM_LIMIT),
-        name="reduce",
-    )(slots, subs, recv_coarse, down_weight)
+        compiler_params=pltpu.CompilerParams(
+            collective_id=1, has_side_effects=True, vmem_limit_bytes=VMEM_LIMIT
+        ),
+        name="exchange",
+    )(slots, send_sub.reshape(peers, 1, 2 * half), recv_coarse, down_weight)
 
 
 def on_device(
@@ -264,12 +358,10 @@
     features, conv_weight, down_weight, kernel_map, halo_rows, send_rows, send_sub, recv_coarse,
 ):
     voxels, channels = features.shape
-    subs = lax.all_to_all(send_sub, "gx", split_axis=0, concat_axis=0, tiled=True)
     feat_t = features.T
     halo = exchange_halo(feat_t, halo_rows, n_gx, n_gy).reshape(-1, BLOCK)
     refined_t, slots = convolve(feat_t, halo, conv_weight, kernel_map, send_rows)
-    landed = lax.all_to_all(slots, "gx", split_axis=0, concat_axis=0, tiled=True)
-    coarse = reduce_coarse(landed, subs, recv_coarse, down_weight, voxels // 4)
+    coarse = exchange_and_reduce(slots, send_sub, recv_coarse, down_weight, voxels // 4, n_gx)
     return refined_t.T, coarse
 
 

time: 182 us -> 134 us (0.74)
  waiting for transfers between devices: 48.5 us -> 0 us
  Pallas kernels: 107 us -> 131 us
  starting transfers between devices: 20.2 us -> 0 us
    all_to_all x2 -> x0, waiting for transfers between devices: 48.5 us -> none  [the longest x1 48.5 us: on_device(): lax.all_to_all(slots, 'gx', split_axis=0, concat_axis=0, tiled=True)]
    pallas_call x1, Pallas kernels: 45.5 us -> 66.2 us  [exchange_and_reduce(): pl.pallas_call(functools.partial(exchange_kernel, n_gx, depth, window), o...]
    all_to_all x2 -> x0, starting transfers between devices: 20.2 us -> none  [the longest x1 11.6 us: on_device(): lax.all_to_all(send_sub, 'gx', split_axis=0, concat_axis=0, tiled=True)]
    pallas_call x1, Pallas kernels: 15.7 us -> 18.4 us  [exchange_halo(): pl.pallas_call(functools.partial(halo_kernel, n_gx, n_gy), out_shape=jax....]
  transfers between devices with their start and end apart: 2 -> 0, of which waited for: 1 -> 0; matrix products, arithmetic and copies ran while one was open for 0% -> 0% of each run, Pallas kernels for 34% -> 0%
where the time goes in v2:
time: 134 us
  Pallas kernels  131 us (98%)
  local copies, waits for them, and re-layouts  2.55 us (2%)
    pallas_call x1, Pallas kernels, exchange_and_reduce(): pl.pallas_call(functools.partial(exchange_kernel, n_gx, depth, window), o...  66.2 us
    pallas_call x1, Pallas kernels, convolve(): pl.pallas_call(functools.partial(conv_kernel, group), out_shape=(jax.Shap...  43.7 us
    pallas_call x1, Pallas kernels, exchange_halo(): pl.pallas_call(functools.partial(halo_kernel, n_gx, n_gy), out_shape=jax....  18.4 us

profile of v2, /device:TPU:14, one launch (start us, length us, event | category | flops | bytes accessed | tf_op | source)
XLA Modules:
  0.0 134.0 jit_solution(2426895501218244017)
XLA Ops:
  0.6 2.5 %pack.1.sent = bf16[8,512,128]{2,1,0:T(8,128)(2,1)} custom-call(s32[8,8]{1,0:T(8,128)} %halo_ref.1, bf16[64,8192]{1,0:T(8,128)(2,1)} %bitcast.4), custom_call_target="tpu_custom_call" | custom-call | tf_op jit(solution)/shard_map/pack/pallas_call | solution.py:73
  3.2 0.0 copy-start
  3.2 18.4 %halo.1 = bf16[8,512,128]{2,1,0:T(8,128)(2,1)} custom-call(bf16[8,512,128]{2,1,0:T(8,128)(2,1)} %pack.1.sent), custom_call_target="tpu_custom_call" | custom-call | tf_op jit(solution)/shard_map/halo/pallas_call | solution.py:80
  21.5 43.7 %convolve.1 = (bf16[64,8192]{1,0:T(8,128)(2,1)}, bf16[32,256,128]{2,1,0:T(8,128)(2,1)}) custom-call(s32[27,64]{1,0:T(8,128)} %map_ref.1, s32[32,512]{1,0:T(8,128)} %rows_ref.1, bf16[64,8192]{1,0:T(8,128)(2,1)} %bitcast.5, bf16[4096,128]{1,0:T(8,128)(2,1)} %bitcast.6, bf16[1728,64]{1,0:T(8,128)(2,1)} %bitcast.7), custom_call_target="tpu_custom_call" | custom-call | tf_op jit(solution)/shard_map/convolve/pallas_call | solution.py:174
  65.2 0.0 copy-done
  65.2 0.7 reshape.15.sub_ref
  65.9 66.2 %exchange.1 = bf16[2048,128]{1,0:T(8,128)(2,1)} custom-call(bf16[32,256,128]{2,1,0:T(8,128)(2,1)} %get-tuple-element.5.slot_ref, s32[32,1,512]{2,1,0:T(1,128)} %reshape.15.sub_ref, s32[32,512]{1,0:T(8,128)} %coarse_ref.1, bf16[8,64,128]{2,1,0:T(8,128)(2,1)} %w_ref.1), custom_call_target="tpu_custom_call" | custom-call | tf_op jit(solution)/shard_map/exchange/pallas_call | solution.py:330
  132.2 1.9 %copy.11 = bf16[2048,128]{1,0:T(8,128)(2,1)} copy(bf16[2048,128]{1,0:T(8,128)(2,1)} %exchange.1) | data formatting | bytes 1048576
Async XLA Ops:
  3.2 62.1 %copy-start = (s32[32,512]{1,0:T(8,128)S(1)}, s32[32,512]{1,0:T(8,128)}, u32[]{:S(2)}) copy-start(s32[32,512]{1,0:T(8,128)} %param.14) | copy-start | bytes 196612

commit v3 on v2

v3 whole, which is shorter than its diff:
```python
import functools

import jax
import jax.numpy as jnp
from jax import lax
from jax.experimental import pallas as pl
from jax.experimental.pallas import tpu as pltpu
from jax.sharding import PartitionSpec as P

MESH = pl.DeviceIdType.MESH
BLOCK = 128
DIRECTIONS = ((-1, -1), (-1, 0), (-1, 1), (0, -1), (0, 1), (1, -1), (1, 0), (1, 1))
VMEM_LIMIT = 60 * 1024 * 1024


def pack_kernel(halo_ref, feat_ref, out_ref):
    channels = feat_ref.shape[0]
    directions, per_direction = halo_ref.shape

    @pl.loop(0, directions)
    def _(j):
        for m in range(per_direction):
            column = pl.multiple_of(halo_ref[j, m] * BLOCK, BLOCK)
            out_ref[j, m * channels : (m + 1) * channels, :] = feat_ref[:, pl.ds(column, BLOCK)]


def halo_kernel(n_gx, n_gy, sent, out_ref, send_sem, recv_sem):
    gx, gy = lax.axis_index("gx"), lax.axis_index("gy")
    barrier = pltpu.get_barrier_semaphore()
    for dx, dy in DIRECTIONS:
        peer = (lax.rem(gx + dx + n_gx, n_gx), lax.rem(gy + dy + n_gy, n_gy))
        pl.semaphore_signal(barrier, inc=1, device_id=peer, device_id_type=MESH)
    pl.semaphore_wait(barrier, len(DIRECTIONS))

    def inside(x, y):
        return (x >= 0) & (x < n_gx) & (y >= 0) & (y < n_gy)

    def copy(j, peer):
        return pltpu.make_async_remote_copy(
            src_ref=sent.at[j],
            dst_ref=out_ref.at[j],
            send_sem=send_sem.at[j],
            recv_sem=recv_sem.at[j],
            device_id=peer,
            device_id_type=MESH,
        )

    for j, (dx, dy) in enumerate(DIRECTIONS):
        @pl.when(inside(gx + dx, gy + dy))
        def _():
            copy(j, (gx + dx, gy + dy)).start()

    for j, (dx, dy) in enumerate(DIRECTIONS):
        @pl.when(jnp.logical_not(inside(gx - dx, gy - dy)))
        def _():
            out_ref[j] = jnp.zeros(out_ref.shape[1:], out_ref.dtype)

    for j, (dx, dy) in enumerate(DIRECTIONS):
        @pl.when(inside(gx - dx, gy - dy))
        def _():
            copy(j, (gx, gy)).wait_recv()

        @pl.when(inside(gx + dx, gy + dy))
        def _():
            copy(j, (gx, gy)).wait_send()


def exchange_halo(feat_t, halo_rows, n_gx, n_gy):
    channels = feat_t.shape[0]
    directions, per_direction = halo_rows.shape
    page = (directions, per_direction * channels, BLOCK)
    vmem = pl.BlockSpec(memory_space=pltpu.VMEM)
    sent = pl.pallas_call(
        pack_kernel,
        out_shape=jax.ShapeDtypeStruct(page, feat_t.dtype),
        in_specs=[pl.BlockSpec(memory_space=pltpu.SMEM), vmem],
        out_specs=vmem,
        name="pack",
    )(halo_rows, feat_t)
    return pl.pallas_call(
        functools.partial(halo_kernel, n_gx, n_gy),
        out_shape=jax.ShapeDtypeStruct(page, feat_t.dtype),
        in_specs=[vmem],
        out_specs=vmem,
        scratch_shapes=[
            pltpu.SemaphoreType.DMA((directions,)),
            pltpu.SemaphoreType.DMA((directions,)),
        ],
        compiler_params=pltpu.CompilerParams(collective_id=0, has_side_effects=True),
        name="halo",
    )(sent)


def doubled_rows(block):
    wide = jnp.concatenate([block, block], axis=0)
    return jnp.transpose(wide)


def conv_kernel(
    group, map_ref, feat_ref, halo_ref, conv_ref, fine_out, fine, table, weights, lhs
):
    offsets, blocks = map_ref.shape
    channels, voxels = feat_ref.shape
    halo_blocks = halo_ref.shape[0] // channels
    lanes = fine.shape[1]
    pairs = (offsets + 1) // 2

    weights[...] = jnp.zeros(weights.shape, weights.dtype)
    weights[: offsets * channels, :] = jnp.concatenate([conv_ref[...], conv_ref[...]], axis=1)

    @pl.loop(0, blocks)
    def _(i):
        column = pl.multiple_of(i * BLOCK, BLOCK)
        table[pl.ds(column, BLOCK), :] = doubled_rows(feat_ref[:, pl.ds(column, BLOCK)])

    @pl.loop(0, halo_blocks)
    def _(i):
        row = pl.multiple_of((blocks + i) * BLOCK, BLOCK)
        start = pl.multiple_of(i * channels, channels)
        table[pl.ds(row, BLOCK), :] = doubled_rows(halo_ref[pl.ds(start, channels), :])

    empty = (blocks + halo_blocks) * BLOCK
    table[empty : empty + BLOCK, :] = jnp.zeros((BLOCK, lanes), table.dtype)
    fine[voxels : voxels + 8, :] = jnp.zeros((8, lanes), fine.dtype)

    low = lax.broadcasted_iota(jnp.int32, (BLOCK, lanes), 1) < channels

    def pick(k, i):
        return table[pl.ds(pl.multiple_of(map_ref[k, i] * BLOCK, BLOCK), BLOCK), :]

    @pl.loop(0, blocks // group)
    def _(g):
        for b in range(group):
            i = g * group + b
            for pair in range(pairs):
                first = pick(2 * pair, i)
                if 2 * pair + 1 < offsets:
                    both = jnp.where(low, first, pick(2 * pair + 1, i))
                else:
                    both = jnp.where(low, first, jnp.zeros_like(first))
                lhs[b * BLOCK : (b + 1) * BLOCK, pair * lanes : (pair + 1) * lanes] = both
        summed = jnp.dot(lhs[...], weights[...], preferred_element_type=jnp.float32)
        refined = jnp.maximum(summed, 0.0).astype(jnp.bfloat16).astype(jnp.float32)
        start = pl.multiple_of(g * group * BLOCK, group * BLOCK)
        fine[pl.ds(start, group * BLOCK), :] = refined
        for b in range(group):
            block = refined[b * BLOCK : (b + 1) * BLOCK, :]
            column = pl.multiple_of(start + b * BLOCK, BLOCK)
            fine_out[:, pl.ds(column, BLOCK)] = jnp.transpose(block)[:channels, :].astype(
                fine_out.dtype
            )

def convolve(feat_t, halo, conv_weight, kernel_map):
    channels, voxels = feat_t.shape
    offsets, blocks = kernel_map.shape
    group = 8
    pairs = (offsets + 1) // 2
    lanes = 2 * channels
    halo_blocks = halo.shape[0] // channels
    vmem = pl.BlockSpec(memory_space=pltpu.VMEM)
    return pl.pallas_call(
        functools.partial(conv_kernel, group),
        out_shape=(
            jax.ShapeDtypeStruct((channels, voxels), jnp.bfloat16),
            jax.ShapeDtypeStruct((voxels + 8, lanes), jnp.float32),
        ),
        in_specs=[pl.BlockSpec(memory_space=pltpu.SMEM), vmem, vmem, vmem],
        out_specs=(vmem, vmem),
        scratch_shapes=[
            pltpu.VMEM(((blocks + halo_blocks + 1) * BLOCK, lanes), jnp.bfloat16),
            pltpu.VMEM((pairs * lanes, lanes), jnp.bfloat16),
            pltpu.VMEM((group * BLOCK, pairs * lanes), jnp.bfloat16),
        ],
        compiler_params=pltpu.CompilerParams(vmem_limit_bytes=VMEM_LIMIT),
        name="convolve",
    )(kernel_map, feat_t, halo, conv_weight.reshape(offsets * channels, channels))


def torus_peer(me, depth, n_gx, step):
    spread = lax.rem(step, depth)
    odd = lax.rem(spread, 2)
    ahead = odd * ((spread + 1) // 2) + (1 - odd) * (depth - spread // 2)
    across, along = me // depth, lax.rem(me, depth)
    wide = n_gx // depth
    there = lax.rem(across + step // depth, wide)
    back = lax.rem(across - step // depth + wide, wide)
    to = there * depth + lax.rem(along + ahead, depth)
    source = back * depth + lax.rem(along - ahead + depth, depth)
    return to, source


def exchange_kernel(
    n_gx, depth, ahead,
    rows_ref, fine, sub_ref, coarse_ref, down_ref, coarse_out,
    stage, packed, own_codes,
    landed, codes, wide, placed, terms, hot, total,
    row_send, row_recv, code_send, code_recv,
):
    me, gy = lax.axis_index("gx"), lax.axis_index("gy")
    peers, half, lanes = packed.shape
    capacity = 2 * half
    subs, channels, width = down_ref.shape
    coarse_count = coarse_out.shape[0]
    zero, one = jnp.bfloat16(0), jnp.bfloat16(1)

    barrier = pltpu.get_barrier_semaphore()

    @pl.loop(1, n_gx)
    def _(step):
        to, source = torus_peer(me, depth, n_gx, step)
        pl.semaphore_signal(barrier, inc=1, device_id=(to, gy), device_id_type=MESH)

    wide[...] = jnp.zeros(wide.shape, wide.dtype)
    for s in range(subs):
        wide[s * lanes : s * lanes + channels, :width] = down_ref[s]
        wide[s * lanes + channels : (s + 1) * lanes, width:] = down_ref[s]
    total[...] = jnp.zeros(total.shape, total.dtype)
    for p in range(peers):
        own_codes[p] = sub_ref[p : p + 1, :]

    low_row = lax.broadcasted_iota(jnp.int32, (1, lanes), 1) < channels
    low_half = lax.broadcasted_iota(jnp.int32, (half, lanes), 1) < channels
    ids = lax.broadcasted_iota(jnp.int32, (BLOCK, capacity), 0).astype(jnp.bfloat16)

    def gather(step):
        to, source = torus_peer(me, depth, n_gx, step)
        base = to * capacity
        for c in range(half):
            first = fine[pl.ds(rows_ref[base + c], 1), :]
            second = fine[pl.ds(rows_ref[base + half + c], 1), :]
            stage[c : c + 1, :] = jnp.where(low_row, first, second)
        packed[step] = stage[...].astype(packed.dtype)

    def rows_copy(step, to):
        return pltpu.make_async_remote_copy(
            src_ref=packed.at[step],
            dst_ref=landed.at[step],
            send_sem=row_send.at[step],
            recv_sem=row_recv.at[step],
            device_id=(to, gy),
            device_id_type=MESH,
        )

    def codes_copy(step, to):
        return pltpu.make_async_remote_copy(
            src_ref=own_codes.at[to],
            dst_ref=codes.at[step],
            send_sem=code_send.at[step],
            recv_sem=code_recv.at[step],
            device_id=(to, gy),
            device_id_type=MESH,
        )

    def send(step):
        to, source = torus_peer(me, depth, n_gx, step)
        codes_copy(step, to).start()
        rows_copy(step, to).start()

    def reduce(step, rows, code):
        to, source = torus_peer(me, depth, n_gx, step)
        target = coarse_ref[pl.ds(source, 1), :]
        part = target // BLOCK
        lower = target - part * BLOCK
        upper = part // 8
        part = part - upper * 8
        mark = (code + subs * upper).astype(jnp.float32).astype(jnp.bfloat16)
        first = jnp.transpose(jnp.broadcast_to(mark[:, :half], (lanes, half)))
        second = jnp.transpose(jnp.broadcast_to(mark[:, half:], (lanes, half)))
        edge = jnp.bfloat16(subs)
        first_up, second_up = first >= edge, second >= edge
        column = jnp.where(
            low_half,
            jnp.where(first_up, first - edge, first),
            jnp.where(second_up, second - edge, second),
        )
        for s in range(subs):
            placed[:, s * lanes : (s + 1) * lanes] = jnp.where(
                column == jnp.bfloat16(s), rows, jnp.zeros_like(rows)
            )
        product = jnp.dot(placed[...], wide[...], preferred_element_type=jnp.float32)
        product = product.astype(jnp.bfloat16)
        terms[:half, :width] = jnp.where(first_up, zero, product[:, :width])
        terms[:half, width:] = jnp.where(first_up, product[:, :width], zero)
        terms[half:, :width] = jnp.where(second_up, zero, product[:, width:])
        terms[half:, width:] = jnp.where(second_up, product[:, width:], zero)
        for h in range(coarse_count // 2 // BLOCK):
            wanted = jnp.where(part == h, lower, -1).astype(jnp.float32).astype(jnp.bfloat16)
            hot[h * BLOCK : (h + 1) * BLOCK, :] = jnp.where(ids == wanted, one, zero)
        total[...] += jnp.dot(hot[...], terms[...], preferred_element_type=jnp.float32)

    pl.semaphore_wait(barrier, n_gx - 1)

    gather(1)

    @pl.loop(2, ahead + 1)
    def _(step):
        gather(step)
        send(step - 1)

    gather(0)
    send(ahead)

    gather(ahead + 1)
    reduce(0, packed[0], own_codes[me])

    @pl.loop(1, n_gx - ahead - 1)
    def _(step):
        send(step + ahead)
        codes_copy(step, me).wait_recv()
        rows_copy(step, me).wait_recv()
        gather(step + ahead + 1)
        reduce(step, landed[step], codes[step])

    send(n_gx - 1)

    @pl.loop(n_gx - ahead - 1, n_gx)
    def _(step):
        codes_copy(step, me).wait_recv()
        rows_copy(step, me).wait_recv()
        reduce(step, landed[step], codes[step])

    coarse_out[: coarse_count // 2, :] = total[:, :width].astype(coarse_out.dtype)
    coarse_out[coarse_count // 2 :, :] = total[:, width:].astype(coarse_out.dtype)

    @pl.loop(1, n_gx)
    def _(step):
        codes_copy(step, me).wait_send()
        rows_copy(step, me).wait_send()


def exchange_and_reduce(fine, down_weight, send_rows, send_sub, recv_coarse, coarse_count, n_gx):
    peers, capacity = send_rows.shape
    subs, channels, width = down_weight.shape
    depth, ahead = 8, 16
    half, lanes = capacity // 2, 2 * channels
    vmem = pl.BlockSpec(memory_space=pltpu.VMEM)
    smem = pl.BlockSpec(memory_space=pltpu.SMEM)
    bf16 = jnp.bfloat16
    return pl.pallas_call(
        functools.partial(exchange_kernel, n_gx, depth, ahead),
        out_shape=jax.ShapeDtypeStruct((coarse_count, width), bf16),
        in_specs=[smem, vmem, vmem, vmem, vmem],
        out_specs=vmem,
        scratch_shapes=[
            pltpu.VMEM((half, lanes), jnp.float32),
            pltpu.VMEM((peers, half, lanes), bf16),
            pltpu.VMEM((peers, 1, capacity), jnp.int32),
            pltpu.VMEM((peers, half, lanes), bf16),
            pltpu.VMEM((peers, 1, capacity), jnp.int32),
            pltpu.VMEM((subs * lanes, 2 * width), bf16),
            pltpu.VMEM((half, subs * lanes), bf16),
            pltpu.VMEM((capacity, 2 * width), bf16),
            pltpu.VMEM((coarse_count // 2, capacity), bf16),
            pltpu.VMEM((coarse_count // 2, 2 * width), jnp.float32),
            pltpu.SemaphoreType.DMA((peers,)),
            pltpu.SemaphoreType.DMA((peers,)),
            pltpu.SemaphoreType.DMA((peers,)),
            pltpu.SemaphoreType.DMA((peers,)),
        ],
        compiler_params=pltpu.CompilerParams(
            collective_id=1, has_side_effects=True, vmem_limit_bytes=VMEM_LIMIT
        ),
        name="exchange",
    )(send_rows.reshape(-1), fine, send_sub, recv_coarse, down_weight)


def on_device(
    n_gx, n_gy,
    features, conv_weight, down_weight, kernel_map, halo_rows, send_rows, send_sub, recv_coarse,
):
    voxels, channels = features.shape
    feat_t = features.T
    halo = exchange_halo(feat_t, halo_rows, n_gx, n_gy).reshape(-1, BLOCK)
    refined_t, fine = convolve(feat_t, halo, conv_weight, kernel_map)
    coarse = exchange_and_reduce(
        fine, down_weight, send_rows, send_sub, recv_coarse, voxels // 4, n_gx
    )
    return refined_t.T, coarse


def solution(mesh):
    split = P(None, ("gx", "gy"))
    return jax.shard_map(
        functools.partial(on_device, mesh.shape["gx"], mesh.shape["gy"]),
        mesh=mesh,
        in_specs=(P(("gx", "gy"), None), P(), P(), split, split, split, split, split),
        out_specs=(P(("gx", "gy"), None), P(("gx", "gy"), None)),
        check_vma=False,
    )
```

time: 134 us -> 119 us (0.89)
  Pallas kernels: 131 us -> 116 us
    pallas_call x1, Pallas kernels: 43.7 us -> 27.3 us  [convolve(): pl.pallas_call(functools.partial(conv_kernel, group), out_shape=(jax.Shap...]
where the time goes in v3:
time: 119 us
  Pallas kernels  116 us (97%)
  local copies, waits for them, and re-layouts  2.52 us (2%)
    pallas_call x1, Pallas kernels, exchange_and_reduce(): pl.pallas_call(functools.partial(exchange_kernel, n_gx, depth, ahead), ou...  67.3 us
    pallas_call x1, Pallas kernels, convolve(): pl.pallas_call(functools.partial(conv_kernel, group), out_shape=(jax.Shap...  27.3 us
    pallas_call x1, Pallas kernels, exchange_halo(): pl.pallas_call(functools.partial(halo_kernel, n_gx, n_gy), out_shape=jax....  18.3 us
    pallas_call x1, Pallas kernels, exchange_halo(): pl.pallas_call(pack_kernel, out_shape=jax.ShapeDtypeStruct(page, feat_t.d...  2.56 us
    unnamed x4, local copies, waits for them, and re-layouts  2.52 us

profile of v3, /device:TPU:14, one launch (start us, length us, event | category | flops | bytes accessed | tf_op | source)
XLA Modules:
  0.0 118.7 jit_solution(6811453063024894646)
XLA Ops:
  0.6 0.0 copy-start
  0.6 2.6 %pack.1.sent = bf16[8,512,128]{2,1,0:T(8,128)(2,1)} custom-call(s32[8,8]{1,0:T(8,128)} %halo_ref.1, bf16[64,8192]{1,0:T(8,128)(2,1)} %bitcast.6), custom_call_target="tpu_custom_call" | custom-call | tf_op jit(solution)/shard_map/pack/pallas_call | solution.py:73
  3.2 18.3 %halo.1 = bf16[8,512,128]{2,1,0:T(8,128)(2,1)} custom-call(bf16[8,512,128]{2,1,0:T(8,128)(2,1)} %pack.1.sent), custom_call_target="tpu_custom_call" | custom-call | tf_op jit(solution)/shard_map/halo/pallas_call | solution.py:80
  21.5 27.3 %convolve.1 = (bf16[64,8192]{1,0:T(8,128)(2,1)}, f32[8200,128]{1,0:T(8,128)}) custom-call(s32[27,64]{1,0:T(8,128)} %map_ref.1, bf16[64,8192]{1,0:T(8,128)(2,1)} %bitcast.7, bf16[4096,128]{1,0:T(8,128)(2,1)} %bitcast.8, bf16[1728,64]{1,0:T(8,128)(2,1)} %bitcast.9), custom_call_target="tpu_custom_call" | custom-call | tf_op jit(solution)/shard_map/convolve/pallas_call | solution.py:161
  48.9 0.0 copy-done
  48.9 0.6 copy.10
  49.5 67.3 %exchange.1 = bf16[2048,128]{1,0:T(8,128)(2,1)} custom-call(s32[16384]{0:T(1024)} %bitcast.10, f32[8200,128]{1,0:T(8,128)} %get-tuple-element.5.fine, s32[32,512]{1,0:T(8,128)} %sub_ref.1, s32[32,512]{1,0:T(8,128)} %coarse_ref.1, bf16[8,64,128]{2,1,0:T(8,128)(2,1)} %down_ref.1), custom_call_target="tpu_custom_call" | custom-call | tf_op jit(solution)/shard_map/exchange/pallas_call | solution.py:339
  116.9 1.9 %copy.12 = bf16[2048,128]{1,0:T(8,128)(2,1)} copy(bf16[2048,128]{1,0:T(8,128)(2,1)} %exchange.1) | data formatting | bytes 1048576
Async XLA Ops:
  0.6 48.2 %copy-start = (s32[32,512]{1,0:T(8,128)S(1)}, s32[32,512]{1,0:T(8,128)}, u32[]{:S(2)}) copy-start(s32[32,512]{1,0:T(8,128)} %param.13) | copy-start | bytes 196612

commit v4 on v3

--- a/solution.py
+++ b/solution.py
@@ -91,70 +91,42 @@
     )(sent)
 
 
-def doubled_rows(block):
-    wide = jnp.concatenate([block, block], axis=0)
-    return jnp.transpose(wide)
-
-
 def conv_kernel(
-    group, map_ref, feat_ref, halo_ref, conv_ref, fine_out, fine, table, weights, lhs
+    group, map_ref, feat_ref, halo_ref, conv_ref, fine_out, fine, table, weights, picked
 ):
     offsets, blocks = map_ref.shape
     channels, voxels = feat_ref.shape
-    halo_blocks = halo_ref.shape[0] // channels
     lanes = fine.shape[1]
-    pairs = (offsets + 1) // 2
-
-    weights[...] = jnp.zeros(weights.shape, weights.dtype)
-    weights[: offsets * channels, :] = jnp.concatenate([conv_ref[...], conv_ref[...]], axis=1)
-
-    @pl.loop(0, blocks)
-    def _(i):
-        column = pl.multiple_of(i * BLOCK, BLOCK)
-        table[pl.ds(column, BLOCK), :] = doubled_rows(feat_ref[:, pl.ds(column, BLOCK)])
-
-    @pl.loop(0, halo_blocks)
-    def _(i):
-        row = pl.multiple_of((blocks + i) * BLOCK, BLOCK)
-        start = pl.multiple_of(i * channels, channels)
-        table[pl.ds(row, BLOCK), :] = doubled_rows(halo_ref[pl.ds(start, channels), :])
-
-    empty = (blocks + halo_blocks) * BLOCK
-    table[empty : empty + BLOCK, :] = jnp.zeros((BLOCK, lanes), table.dtype)
+    weights[...] = jnp.transpose(conv_ref[...])
+    for i in range(blocks):
+        table[i] = feat_ref[:, i * BLOCK : (i + 1) * BLOCK]
+    for i in range(blocks, table.shape[0] - 1):
+        start = (i - blocks) * channels
+        table[i] = halo_ref[start : start + channels, :]
+    table[table.shape[0] - 1] = jnp.zeros(table.shape[1:], table.dtype)
     fine[voxels : voxels + 8, :] = jnp.zeros((8, lanes), fine.dtype)
-
-    low = lax.broadcasted_iota(jnp.int32, (BLOCK, lanes), 1) < channels
-
-    def pick(k, i):
-        return table[pl.ds(pl.multiple_of(map_ref[k, i] * BLOCK, BLOCK), BLOCK), :]
 
     @pl.loop(0, blocks // group)
     def _(g):
+        for k in range(offsets):
+            for b in range(group):
+                picked[k * channels : (k + 1) * channels, b * BLOCK : (b + 1) * BLOCK] = table[
+                    map_ref[k, g * group + b]
+                ]
+        summed = jnp.dot(weights[...], picked[...], preferred_element_type=jnp.float32)
+        refined = jnp.maximum(summed, 0.0).astype(jnp.bfloat16)
+        start = pl.multiple_of(g * group * BLOCK, group * BLOCK)
+        fine_out[:, pl.ds(start, group * BLOCK)] = refined
         for b in range(group):
-            i = g * group + b
-            for pair in range(pairs):
-                first = pick(2 * pair, i)
-                if 2 * pair + 1 < offsets:
-                    both = jnp.where(low, first, pick(2 * pair + 1, i))
-                else:
-                    both = jnp.where(low, first, jnp.zeros_like(first))
-                lhs[b * BLOCK : (b + 1) * BLOCK, pair * lanes : (pair + 1) * lanes] = both
-        summed = jnp.dot(lhs[...], weights[...], preferred_element_type=jnp.float32)
-        refined = jnp.maximum(summed, 0.0).astype(jnp.bfloat16).astype(jnp.float32)
-        start = pl.multiple_of(g * group * BLOCK, group * BLOCK)
-        fine[pl.ds(start, group * BLOCK), :] = refined
-        for b in range(group):
-            block = refined[b * BLOCK : (b + 1) * BLOCK, :]
-            column = pl.multiple_of(start + b * BLOCK, BLOCK)
-            fine_out[:, pl.ds(column, BLOCK)] = jnp.transpose(block)[:channels, :].astype(
-                fine_out.dtype
-            )
+            block = refined[:, b * BLOCK : (b + 1) * BLOCK].astype(jnp.float32)
+            row = pl.multiple_of(start + b * BLOCK, BLOCK)
+            fine[pl.ds(row, BLOCK), :] = jnp.transpose(jnp.concatenate([block, block], axis=0))
+
 
 def convolve(feat_t, halo, conv_weight, kernel_map):
     channels, voxels = feat_t.shape
     offsets, blocks = kernel_map.shape
-    group = 8
-    pairs = (offsets + 1) // 2
+    group = 32
     lanes = 2 * channels
     halo_blocks = halo.shape[0] // channels
     vmem = pl.BlockSpec(memory_space=pltpu.VMEM)
@@ -167,9 +139,9 @@
         in_specs=[pl.BlockSpec(memory_space=pltpu.SMEM), vmem, vmem, vmem],
         out_specs=(vmem, vmem),
         scratch_shapes=[
-            pltpu.VMEM(((blocks + halo_blocks + 1) * BLOCK, lanes), jnp.bfloat16),
-            pltpu.VMEM((pairs * lanes, lanes), jnp.bfloat16),
-            pltpu.VMEM((group * BLOCK, pairs * lanes), jnp.bfloat16),
+            pltpu.VMEM((blocks + halo_blocks + 1, channels, BLOCK), jnp.bfloat16),
+            pltpu.VMEM((channels, offsets * channels), jnp.bfloat16),
+            pltpu.VMEM((offsets * channels, group * BLOCK), jnp.bfloat16),
         ],
         compiler_params=pltpu.CompilerParams(vmem_limit_bytes=VMEM_LIMIT),
         name="convolve",

time: 119 us -> 104 us (0.87)
  Pallas kernels: 116 us -> 101 us
    pallas_call x1, Pallas kernels: 27.3 us -> 12.5 us  [convolve(): pl.pallas_call(functools.partial(conv_kernel, group), out_shape=(jax.Shap...]
where the time goes in v4:
time: 104 us
  Pallas kernels  101 us (97%)
  local copies, waits for them, and re-layouts  2.52 us (2%)
    pallas_call x1, Pallas kernels, exchange_and_reduce(): pl.pallas_call(functools.partial(exchange_kernel, n_gx, depth, ahead), ou...  67.3 us
    pallas_call x1, Pallas kernels, exchange_halo(): pl.pallas_call(functools.partial(halo_kernel, n_gx, n_gy), out_shape=jax....  18.3 us
    pallas_call x1, Pallas kernels, convolve(): pl.pallas_call(functools.partial(conv_kernel, group), out_shape=(jax.Shap...  12.5 us
    pallas_call x1, Pallas kernels, exchange_halo(): pl.pallas_call(pack_kernel, out_shape=jax.ShapeDtypeStruct(page, feat_t.d...  2.56 us
    unnamed x4, local copies, waits for them, and re-layouts  2.52 us

profile of v4, /device:TPU:14, one launch (start us, length us, event | category | flops | bytes accessed | tf_op | source)
XLA Modules:
  0.0 103.9 jit_solution(2611023567919787418)
XLA Ops:
  0.6 0.0 copy-start
  0.6 2.6 %pack.1.sent = bf16[8,512,128]{2,1,0:T(8,128)(2,1)} custom-call(s32[8,8]{1,0:T(8,128)} %halo_ref.1, bf16[64,8192]{1,0:T(8,128)(2,1)} %bitcast.6), custom_call_target="tpu_custom_call" | custom-call | tf_op jit(solution)/shard_map/pack/pallas_call | solution.py:73
  3.2 18.3 %halo.1 = bf16[8,512,128]{2,1,0:T(8,128)(2,1)} custom-call(bf16[8,512,128]{2,1,0:T(8,128)(2,1)} %pack.1.sent), custom_call_target="tpu_custom_call" | custom-call | tf_op jit(solution)/shard_map/halo/pallas_call | solution.py:80
  21.5 12.5 %convolve.1 = (bf16[64,8192]{1,0:T(8,128)(2,1)}, f32[8200,128]{1,0:T(8,128)}) custom-call(s32[27,64]{1,0:T(8,128)} %map_ref.1, bf16[64,8192]{1,0:T(8,128)(2,1)} %bitcast.7, bf16[4096,128]{1,0:T(8,128)(2,1)} %bitcast.8, bf16[1728,64]{1,0:T(8,128)(2,1)} %bitcast.9), custom_call_target="tpu_custom_call" | custom-call | tf_op jit(solution)/shard_map/convolve/pallas_call | solution.py:133
  34.0 0.0 copy-done
  34.0 0.6 copy.10
  34.7 67.3 %exchange.1 = bf16[2048,128]{1,0:T(8,128)(2,1)} custom-call(s32[16384]{0:T(1024)} %bitcast.10, f32[8200,128]{1,0:T(8,128)} %get-tuple-element.5.fine, s32[32,512]{1,0:T(8,128)} %sub_ref.1, s32[32,512]{1,0:T(8,128)} %coarse_ref.1, bf16[8,64,128]{2,1,0:T(8,128)(2,1)} %down_ref.1), custom_call_target="tpu_custom_call" | custom-call | tf_op jit(solution)/shard_map/exchange/pallas_call | solution.py:311
  102.0 1.9 %copy.12 = bf16[2048,128]{1,0:T(8,128)(2,1)} copy(bf16[2048,128]{1,0:T(8,128)(2,1)} %exchange.1) | data formatting | bytes 1048576
Async XLA Ops:
  0.6 33.4 %copy-start = (s32[32,512]{1,0:T(8,128)S(1)}, s32[32,512]{1,0:T(8,128)}, u32[]{:S(2)}) copy-start(s32[32,512]{1,0:T(8,128)} %param.13) | copy-start | bytes 196612
